TPU v7x, 256 devices: a whole 4x4x8 slice. The times are simulated.
256 devices in a mesh: dp: 8 (over x, core), expert: 32 (over z, y).
Axes of the slice: x: 4, y: 4, z: 8, core: 2. Of those that a mesh axis runs over, the one named last changes fastest.
Arguments:
- tokens: bfloat16 [32768, 2048], P(('dp', 'expert')), may hold values from -6 to 6
- routes: int32 [32768, 2], P(('dp', 'expert')), may hold values from 0 to 31, all different within a row; in each aligned block of 128 rows (0 to 127, 128 to 255, ...) at most 12 rows name the same one
- gates: float32 [32768, 2], P(('dp', 'expert')), may hold values from 0.25 to 1
- keep: int32 [32768], P(('dp', 'expert')), may hold values 0 or 1
- cotangent: bfloat16 [32768, 2048], P(('dp', 'expert')), may hold values from -6 to 6
- w_gate: bfloat16 [32, 2048, 768], P('expert'), may hold values from -0.125 to 0.125
- w_up: bfloat16 [32, 2048, 768], P('expert'), may hold values from -0.125 to 0.125
- w_down: bfloat16 [32, 768, 2048], P('expert'), may hold values from -0.21875 to 0.21875
Outputs:
- token_grads: bfloat16 [32768, 2048], P(('dp', 'expert'))
- expert_grads: float32 [32, 2048, 2304], P('expert', 'dp')
Inputs may be any that keep to these rules, and one draw needn't show every extreme that they name: `routes`: the 2 experts of a token differ. Among the 128 tokens of one device, no expert is named more than 12 times, a bound that some block reaches.
All inputs are finite; a program needn't handle non-finite values. No bound on the sum of `keep` on one device may be relied on, other than what follows from the above.
Results may differ from a plain program's by a relative error of at most 0.0061.
Values may be sent and summed in bfloat16 or wider, within the bound.
A program may use at most 128 MiB of HBM per device.

v0:
```python
import jax
import jax.numpy as jnp
from jax import lax
from jax.experimental import pallas as pl
from jax.experimental.pallas import tpu as pltpu
from jax.sharding import PartitionSpec as P

MESH = pl.DeviceIdType.MESH
BF = jnp.bfloat16
F32 = jnp.float32
NQ = 4
SELF = 28


def dot(a, b):
    return jnp.dot(a, b, preferred_element_type=F32)


def dot_nt(a, b):
    return lax.dot_general(a, b, (((1,), (1,)), ((), ())), preferred_element_type=F32)


def dot_tn(a, b):
    return lax.dot_general(a, b, (((0,), (0,)), ((), ())), preferred_element_type=F32)


def onehot(mask):
    return jnp.where(mask, 1.0, 0.0).astype(BF)


def iota(shape, axis):
    return lax.broadcasted_iota(jnp.int32, shape, axis)


def loop(n, body):
    def step(i, carry):
        body(i)
        return carry

    lax.fori_loop(0, n, step, 0)


def kernel(
    aux_ref, tok_hbm, cot_hbm, wg_hbm, wu_hbm, wd_hbm,
    otok_hbm, ograd_hbm,
    xall, call, cot, wg, wu, wd, gacc, uacc, hid, gh, gb, ub, locb, tokout,
    lmat, dmat, umat, pmat, sa, ra, sb, rb,
    ownd, owng, s1d, s1g, r1d, r1g, r2d, r2g,
    ld_sem, st_sem, ssem, rsem, s1s, s1r, s2s, s2r,
):
    me = lax.axis_index("expert")
    dp = lax.axis_index("dp")
    z, y = me // 4, me % 4
    xx, core = dp // 2, dp % 2

    def chunk(i):
        return (xx + 1 + i) % 4

    def load(part, q):
        cols = pl.ds(pl.multiple_of(q * 512, 512), 512)
        src, dst = (
            (tok_hbm.at[:, cols], xall.at[q, pl.ds(384, 128)]),
            (wg_hbm.at[cols], wg.at[q]),
            (wu_hbm.at[cols], wu.at[q]),
            (wd_hbm.at[:, cols], wd.at[q]),
            (cot_hbm.at[:, cols], cot.at[q]),
        )[part]
        return pltpu.make_async_copy(src, dst, ld_sem.at[part, q])

    for part in range(5):
        for i in range(NQ):
            load(part, chunk(i)).start()

    bar = pltpu.get_barrier_semaphore()
    for i in range(1, 32):
        pl.semaphore_signal(bar, inc=1, device_id={"expert": (me + i) % 32}, device_id_type=MESH)
    for i in range(1, 4):
        pl.semaphore_signal(bar, inc=1, device_id={"dp": ((xx + i) % 4) * 2 + core}, device_id_type=MESH)
    pl.semaphore_signal(bar, inc=1, device_id={"dp": xx * 2 + 1 - core}, device_id_type=MESH)

    aux = aux_ref[...]
    lanes = iota((128, 128), 1)
    subs = iota((128, 128), 0)
    eye = lanes == subs
    experts = [aux[:, k : k + 1].astype(jnp.int32) for k in range(2)]
    hots = [onehot(lanes == e) for e in experts]
    before = dot(onehot(lanes < subs), hots[0] + hots[1])
    for k in range(2):
        e = experts[k]
        s = jnp.sum(before * hots[k].astype(F32), axis=1, keepdims=True).astype(jnp.int32)
        dz = ((e >> 2) - z) & 7
        dy = ((e & 3) - y) & 3
        base = (((3 * dz + 7) & 7) * 4 + dy) * 16
        targets = [base + s]
        for j in range(3):
            targets.append(jnp.where((s >> 2) == j, base + 12 + (s & 3), -1))
        rows = []
        for t in range(4):
            dmat[t, pl.ds(128 * k, 128), :] = onehot(iota((128, 512), 1) == targets[t])
            spread = jnp.where(eye, targets[t].astype(F32), 0.0)
            rows.append(jnp.sum(spread, axis=0, keepdims=True).astype(jnp.int32))
        for j in range(3):
            lmat[j, :, pl.ds(256 * k, 128)] = onehot(iota((512, 128), 0) == rows[0])
            lmat[j, :, pl.ds(256 * k + 128, 128)] = onehot(iota((512, 128), 0) == rows[1 + j])

    def exchange(src, dst, a, q, sign):
        for p in range(32):
            m, dy = p // 4, p % 4
            dz = (3 * m + 3) % 8
            block = pl.ds(16 * p, 16)
            if p == SELF:
                pltpu.make_async_copy(src.at[q, block], dst.at[q, block], rsem.at[a, q]).start()
            else:
                to = ((z + sign * dz + 8) % 8) * 4 + (y + sign * dy + 4) % 4
                pltpu.make_async_remote_copy(
                    src_ref=src.at[q, block], dst_ref=dst.at[q, block],
                    send_sem=ssem.at[a, q], recv_sem=rsem.at[a, q],
                    device_id={"expert": to}, device_id_type=MESH,
                ).start()

    def arrived(dst, a, q):
        pltpu.make_async_copy(dst.at[q], dst.at[q], rsem.at[a, q]).wait()

    def sent(src, a, q):
        part = src.at[q, pl.ds(0, 496)]
        pltpu.make_async_copy(part, part, ssem.at[a, q]).wait()

    def scatter(dst, q, first, second):
        for j in range(3):
            part = slice(128 * j, 128 * j + 128)
            stack = jnp.concatenate(
                [first[:, part], first[:, 384:], second[:, part], second[:, 384:]], axis=0
            )
            dst[q, :, part] = dot(lmat[j], stack).astype(BF)

    def gather(mat, src, q):
        main = dot(mat[0], src[q])
        last = dot(mat[1], src[q, :, 0:128])
        last += dot(mat[2], src[q, :, 128:256])
        last += dot(mat[3], src[q, :, 256:384])
        return main, last

    pl.semaphore_wait(bar, 35)

    def dispatch(i):
        q = chunk(i)
        load(0, q).wait()
        rows = xall[q, 384:512, :]
        scatter(sa, q, rows, rows)
        exchange(sa, ra, 0, q, 1)

    loop(NQ, dispatch)

    row = iota((384, 512), 0)
    col = iota((384, 512), 1)
    blk = (row * 43691) >> 19
    s = row - 12 * blk
    umat[0] = onehot(col == 16 * blk + s)
    for j in range(3):
        umat[1 + j] = onehot((col == 16 * blk + 12 + (s & 3)) & ((s >> 2) == j))
    row = iota((512, 384), 0)
    col = iota((512, 384), 1)
    s = row & 15
    pmat[0] = onehot((s < 12) & (col == 12 * (row >> 4) + s))
    for j in range(3):
        pmat[1 + j] = onehot((s >= 12) & (col == 12 * (row >> 4) + 4 * j + s - 12))

    def pack(dst, q, main, last):
        for j in range(3):
            part = slice(128 * j, 128 * j + 128)
            dst[q, :, part] = (dot(pmat[0], main[:, part]) + dot(pmat[1 + j], last)).astype(BF)

    gacc[...] = jnp.zeros_like(gacc)
    uacc[...] = jnp.zeros_like(uacc)

    def forward_in(i):
        q = chunk(i)
        load(1, q).wait()
        load(2, q).wait()
        arrived(ra, 0, q)
        main, last = gather(umat, ra, q)
        xall[q, 0:384, 0:384] = main.astype(BF)
        xall[q, 0:384, 384:512] = last.astype(BF)
        gacc[...] += dot(xall[q], wg[q])
        uacc[...] += dot(xall[q], wu[q])

    loop(NQ, forward_in)

    def activate(r):
        rows = pl.ds(pl.multiple_of(r * 64, 64), 64)
        act = gacc[rows, :]
        hid[rows, :] = (act * jax.nn.sigmoid(act) * uacc[rows, :]).astype(BF)

    loop(8, activate)

    def forward_out(i):
        q = chunk(i)
        load(3, q).wait()
        result = dot(hid[0:384, :], wd[q]).astype(BF)
        pack(sb, q, result[:, 0:384], result[:, 384:512])
        exchange(sb, rb, 1, q, -1)

    loop(NQ, forward_out)

    gates = [aux[:, 2 + k : 3 + k] for k in range(2)]
    keep = aux[:, 4:5]

    def turn(i):
        q = chunk(i)
        load(4, q).wait()
        local = keep * dot(hid[384:512, :], wd[q])
        sent(sa, 0, q)
        arrived(rb, 1, q)
        main, last = gather(dmat, rb, q)
        picked = jnp.concatenate([main, last], axis=1)
        mixed = gates[0] * picked[0:128] + gates[1] * picked[128:256]
        difference = mixed - local
        upstream = cot[q].astype(F32) + difference
        scatter(sa, q, (gates[0] * upstream).astype(BF), (gates[1] * upstream).astype(BF))
        exchange(sa, ra, 2, q, 1)
        call[q, 384:512, :] = (-(keep * difference)).astype(BF)

    loop(NQ, turn)

    gh[...] = jnp.zeros_like(gh)
    mine = pl.ds(pl.multiple_of(core * 256, 256), 256)
    other = pl.ds(pl.multiple_of((1 - core) * 256, 256), 256)

    def to_core(src, dst, part, q):
        return pltpu.make_async_remote_copy(
            src_ref=src.at[q], dst_ref=dst.at[q], send_sem=s1s.at[part, q], recv_sem=s1r.at[part, q],
            device_id={"dp": xx * 2 + 1 - core}, device_id_type=MESH,
        )

    def to_chip(src, dst, part, i):
        return pltpu.make_async_remote_copy(
            src_ref=src.at[chunk(i)], dst_ref=dst.at[2 - i],
            send_sem=s2s.at[part, i], recv_sem=s2r.at[part, 2 - i],
            device_id={"dp": chunk(i) * 2 + core}, device_id_type=MESH,
        )

    def backward_in(i):
        q = chunk(i)
        arrived(ra, 2, q)
        main, last = gather(umat, ra, q)
        call[q, 0:384, 0:384] = main.astype(BF)
        call[q, 0:384, 384:512] = last.astype(BF)
        gh[...] += dot_nt(call[q], wd[q])
        s1d[q] = dot_tn(call[q, :, other], hid[...]).astype(BF)
        to_core(s1d, r1d, 0, q).start()
        ownd[q] = dot_tn(call[q, :, mine], hid[...])

    loop(NQ, backward_in)

    def activate_back(r):
        rows = pl.ds(pl.multiple_of(r * 64, 64), 64)
        act = gacc[rows, :]
        grad = gh[rows, :]
        sigma = jax.nn.sigmoid(act)
        gb[rows, :] = (grad * uacc[rows, :] * (sigma * (1.0 + act * (1.0 - sigma)))).astype(BF)
        ub[rows, :] = (grad * (act * sigma)).astype(BF)

    loop(8, activate_back)

    def backward_out(i):
        q = chunk(i)
        sent(sb, 1, q)
        back = dot_nt(gb[...], wg[q]) + dot_nt(ub[...], wu[q])
        routed = back[0:384].astype(BF)
        pack(sb, q, routed[:, 0:384], routed[:, 384:512])
        exchange(sb, rb, 3, q, -1)
        locb[q] = back[384:512]

    loop(NQ, backward_out)

    def pass_on(own, recv, dst, part, i):
        q = chunk(i)
        to_core(recv, recv, part, q).wait_recv()
        recv[q] = (own[q] + recv[q].astype(F32)).astype(BF)
        to_chip(recv, dst, part, i).start()

    loop(3, lambda i: pass_on(ownd, r1d, r2d, 0, i))

    def weight_grads(i):
        q = chunk(i)
        away = xall[q, :, other]
        s1g[q, :, 0:768] = dot_tn(away, gb[...]).astype(BF)
        s1g[q, :, 768:1536] = dot_tn(away, ub[...]).astype(BF)
        to_core(s1g, r1g, 1, q).start()
        here = xall[q, :, mine]
        owng[q, :, 0:768] = dot_tn(here, gb[...])
        owng[q, :, 768:1536] = dot_tn(here, ub[...])

        @pl.when(i > 0)
        def _():
            pass_on(owng, r1g, r2g, 1, i - 1)

    loop(NQ, weight_grads)

    def finish(i):
        q = chunk(i)
        arrived(rb, 3, q)
        main, last = gather(dmat, rb, q)
        picked = jnp.concatenate([main, last], axis=1)
        tokout[q] = (picked[0:128] + picked[128:256] + locb[q]).astype(BF)
        cols = pl.ds(pl.multiple_of(q * 512, 512), 512)
        pltpu.make_async_copy(tokout.at[q], otok_hbm.at[:, cols], st_sem.at[q]).start()

    loop(NQ, finish)

    def total(own, recv, got, part):
        to_core(recv, recv, part, xx).wait_recv()
        own[xx] = own[xx] + recv[xx].astype(F32)
        for i in range(3):
            to_chip(recv, got, part, i).wait_recv()
        own[xx] = (own[xx] + got[0].astype(F32) + got[1].astype(F32) + got[2].astype(F32)) * 0.125

    total(ownd, r1d, r2d, 0)
    out_d = pltpu.make_async_copy(ownd.at[xx], ograd_hbm.at[:, pl.ds(1536, 768)], st_sem.at[4])
    out_d.start()
    total(owng, r1g, r2g, 1)
    out_g = pltpu.make_async_copy(owng.at[xx], ograd_hbm.at[:, pl.ds(0, 1536)], st_sem.at[5])
    out_g.start()

    def drain(i):
        q = chunk(i)
        sent(sa, 2, q)
        sent(sb, 3, q)
        to_core(s1d, r1d, 0, q).wait_send()
        to_core(s1g, r1g, 1, q).wait_send()
        cols = pl.ds(pl.multiple_of(q * 512, 512), 512)
        pltpu.make_async_copy(tokout.at[q], otok_hbm.at[:, cols], st_sem.at[q]).wait()

    loop(NQ, drain)
    for i in range(3):
        to_chip(r1d, r2d, 0, i).wait_send()
        to_chip(r1g, r2g, 1, i).wait_send()
    out_d.wait()
    out_g.wait()


def on_device(tokens, routes, gates, keep, cotangent, w_gate, w_up, w_down):
    aux = jnp.concatenate(
        [routes.astype(F32), gates, keep.astype(F32)[:, None]], axis=1
    )
    hbm = pl.BlockSpec(memory_space=pl.ANY)
    vmem = pl.BlockSpec(memory_space=pltpu.VMEM)
    sem = pltpu.SemaphoreType.DMA
    token_grads, expert_grads = pl.pallas_call(
        kernel,
        out_shape=(
            jax.ShapeDtypeStruct((128, 2048), BF),
            jax.ShapeDtypeStruct((256, 2304), F32),
        ),
        in_specs=[vmem] + [hbm] * 5,
        out_specs=(hbm, hbm),
        scratch_shapes=[
            pltpu.VMEM((4, 512, 512), BF),
            pltpu.VMEM((4, 512, 512), BF),
            pltpu.VMEM((4, 128, 512), BF),
            pltpu.VMEM((4, 512, 768), BF),
            pltpu.VMEM((4, 512, 768), BF),
            pltpu.VMEM((4, 768, 512), BF),
            pltpu.VMEM((512, 768), F32),
            pltpu.VMEM((512, 768), F32),
            pltpu.VMEM((512, 768), BF),
            pltpu.VMEM((512, 768), F32),
            pltpu.VMEM((512, 768), BF),
            pltpu.VMEM((512, 768), BF),
            pltpu.VMEM((4, 128, 512), F32),
            pltpu.VMEM((4, 128, 512), BF),
            pltpu.VMEM((3, 512, 512), BF),
            pltpu.VMEM((4, 256, 512), BF),
            pltpu.VMEM((4, 384, 512), BF),
            pltpu.VMEM((4, 512, 384), BF),
            pltpu.VMEM((4, 512, 384), BF),
            pltpu.VMEM((4, 512, 384), BF),
            pltpu.VMEM((4, 512, 384), BF),
            pltpu.VMEM((4, 512, 384), BF),
            pltpu.VMEM((4, 256, 768), F32),
            pltpu.VMEM((4, 256, 1536), F32),
            pltpu.VMEM((4, 256, 768), BF),
            pltpu.VMEM((4, 256, 1536), BF),
            pltpu.VMEM((4, 256, 768), BF),
            pltpu.VMEM((4, 256, 1536), BF),
            pltpu.VMEM((3, 256, 768), BF),
            pltpu.VMEM((3, 256, 1536), BF),
            sem((5, 4)), sem((6,)), sem((4, 4)), sem((4, 4)),
            sem((2, 4)), sem((2, 4)), sem((2, 3)), sem((2, 3)),
        ],
        compiler_params=pltpu.CompilerParams(
            collective_id=0, has_side_effects=True, vmem_limit_bytes=67043328
        ),
    )(aux, tokens, cotangent, w_gate[0], w_up[0], w_down[0])
    return token_grads, expert_grads[None]


def solution(mesh):
    return jax.shard_map(
        on_device,
        mesh=mesh,
        in_specs=(
            P(("dp", "expert"), None),
            P(("dp", "expert"), None),
            P(("dp", "expert"), None),
            P(("dp", "expert")),
            P(("dp", "expert"), None),
            P("expert", None, None),
            P("expert", None, None),
            P("expert", None, None),
        ),
        out_specs=(P(("dp", "expert"), None), P("expert", "dp", None)),
        check_vma=False,
    )
```

profile of v0, /device:TPU:6, one launch (start us, length us, event | category | flops | bytes accessed | tf_op | source)
XLA Modules:
  0.0 193.7 jit_solution(10758337589567740361)
XLA Ops:
  0.6 0.7 convert_bitcast_fusion
  1.3 0.7 convert_element_type.6
  2.0 0.7 pad_maximum_fusion
  2.7 0.7 copy.13.aux_ref
  3.4 185.2 %shard_map.95 = (bf16[128,2048]{1,0:T(8,128)(2,1)}, f32[256,2304]{1,0:T(8,128)}) custom-call(f32[128,5]{1,0:T(8,128)} %copy.13.aux_ref, bf16[128,2048]{1,0:T(8,128)(2,1)} %tok_hbm.1, bf16[128,2048]{1,0:T(8,128)(2,1)} %cot_hbm.1, bf16[2048,768]{1,0:T(8,128)(2,1)} %bitcast.6, bf16[2048,768]{1,0:T(8,128)(2,1)} %bitcast.7, bf16[768,2048]{1,0:T(8,128)(2,1)} %bitcast.8), custom_call_target="tpu_custom_call" | custom-call | tf_op jit(solution)/shard_map/pallas_call | solution.py:349
  188.6 1.9 copy.16
  190.5 3.2 %copy.17 = f32[1,256,2304]{2,1,0:T(8,128)} copy(f32[1,256,2304]{2,1,0:T(8,128)} %bitcast.9) | data formatting | bytes 4718592
where the time goes:
time: 195 us; the launch traced here: 194 us
  Pallas kernels  185 us (95%)
  local copies, waits for them, and re-layouts  5.85 us (3%)
  other arithmetic  2.03 us (1%)
    pallas_call x1, Pallas kernels, on_device(): pl.pallas_call(kernel, out_shape=(jax.ShapeDtypeStruct((128, 2048), BF),...  185 us
    unnamed x2, local copies, waits for them, and re-layouts  5.1 us

commit v1 on v0

--- a/solution.py
+++ b/solution.py
@@ -1,3 +1,5 @@
+import functools
+
 import jax
 import jax.numpy as jnp
 from jax import lax
@@ -9,6 +11,7 @@
 BF = jnp.bfloat16
 F32 = jnp.float32
 NQ = 4
+ORDER = (1, 7, 3, 5, 2, 6, 4, 0)
 SELF = 28
 
 
@@ -41,11 +44,11 @@
 
 
 def kernel(
-    aux_ref, tok_hbm, cot_hbm, wg_hbm, wu_hbm, wd_hbm,
+    routes_ref, gates_ref, keep_ref, tok_hbm, cot_hbm, wg_hbm, wu_hbm, wd_hbm,
     otok_hbm, ograd_hbm,
     xall, call, cot, wg, wu, wd, gacc, uacc, hid, gh, gb, ub, locb, tokout,
     lmat, dmat, umat, pmat, sa, ra, sb, rb,
-    ownd, owng, s1d, s1g, r1d, r1g, r2d, r2g,
+    ownd, owng, s1d, s1g, r1d, r1g, r2d, r2g, hd, hg,
     ld_sem, st_sem, ssem, rsem, s1s, s1r, s2s, s2r,
 ):
     me = lax.axis_index("expert")
@@ -54,7 +57,9 @@
     xx, core = dp // 2, dp % 2
 
     def chunk(i):
-        return (xx + 1 + i) % 4
+        if isinstance(i, int):
+            return (xx + (2, 1, 3, 0)[i]) % 4
+        return (xx + jnp.where(i == 0, 2, jnp.where(i == 3, 0, 2 * i - 1))) % 4
 
     def load(part, q):
         cols = pl.ds(pl.multiple_of(q * 512, 512), 512)
@@ -78,11 +83,14 @@
         pl.semaphore_signal(bar, inc=1, device_id={"dp": ((xx + i) % 4) * 2 + core}, device_id_type=MESH)
     pl.semaphore_signal(bar, inc=1, device_id={"dp": xx * 2 + 1 - core}, device_id_type=MESH)
 
-    aux = aux_ref[...]
     lanes = iota((128, 128), 1)
     subs = iota((128, 128), 0)
     eye = lanes == subs
-    experts = [aux[:, k : k + 1].astype(jnp.int32) for k in range(2)]
+
+    def column(row):
+        return jnp.sum(jnp.where(eye, row, jnp.zeros_like(row)), axis=1, keepdims=True)
+
+    experts = [column(routes_ref[k : k + 1, :].astype(F32)).astype(jnp.int32) for k in range(2)]
     hots = [onehot(lanes == e) for e in experts]
     before = dot(onehot(lanes < subs), hots[0] + hots[1])
     for k in range(2):
@@ -90,7 +98,8 @@
         s = jnp.sum(before * hots[k].astype(F32), axis=1, keepdims=True).astype(jnp.int32)
         dz = ((e >> 2) - z) & 7
         dy = ((e & 3) - y) & 3
-        base = (((3 * dz + 7) & 7) * 4 + dy) * 16
+        turn_of = sum(jnp.where(dz == d, m, 0) for m, d in enumerate(ORDER))
+        base = (turn_of * 4 + dy) * 16
         targets = [base + s]
         for j in range(3):
             targets.append(jnp.where((s >> 2) == j, base + 12 + (s & 3), -1))
@@ -105,8 +114,7 @@
 
     def exchange(src, dst, a, q, sign):
         for p in range(32):
-            m, dy = p // 4, p % 4
-            dz = (3 * m + 3) % 8
+            dz, dy = ORDER[p // 4], p % 4
             block = pl.ds(16 * p, 16)
             if p == SELF:
                 pltpu.make_async_copy(src.at[q, block], dst.at[q, block], rsem.at[a, q]).start()
@@ -140,16 +148,15 @@
         last += dot(mat[3], src[q, :, 256:384])
         return main, last
 
-    pl.semaphore_wait(bar, 35)
-
     def dispatch(i):
         q = chunk(i)
         load(0, q).wait()
         rows = xall[q, 384:512, :]
         scatter(sa, q, rows, rows)
-        exchange(sa, ra, 0, q, 1)
 
     loop(NQ, dispatch)
+    pl.semaphore_wait(bar, 35)
+    loop(NQ, lambda i: exchange(sa, ra, 0, chunk(i), 1))
 
     row = iota((384, 512), 0)
     col = iota((384, 512), 1)
@@ -202,8 +209,17 @@
 
     loop(NQ, forward_out)
 
-    gates = [aux[:, 2 + k : 3 + k] for k in range(2)]
-    keep = aux[:, 4:5]
+    def factors(r):
+        rows = pl.ds(pl.multiple_of(r * 64, 64), 64)
+        act = gacc[rows, :]
+        sigma = jax.nn.sigmoid(act)
+        gacc[rows, :] = uacc[rows, :] * (sigma * (1.0 + act * (1.0 - sigma)))
+        uacc[rows, :] = act * sigma
+
+    loop(8, factors)
+
+    gates = [column(gates_ref[k : k + 1, :]) for k in range(2)]
+    keep = column(keep_ref[...].astype(F32))
 
     def turn(i):
         q = chunk(i)
@@ -232,12 +248,45 @@
             device_id={"dp": xx * 2 + 1 - core}, device_id_type=MESH,
         )
 
-    def to_chip(src, dst, part, i):
+    def to_chip(src, dst, part, n, dx):
         return pltpu.make_async_remote_copy(
-            src_ref=src.at[chunk(i)], dst_ref=dst.at[2 - i],
-            send_sem=s2s.at[part, i], recv_sem=s2r.at[part, 2 - i],
-            device_id={"dp": chunk(i) * 2 + core}, device_id_type=MESH,
+            src_ref=src, dst_ref=dst, send_sem=s2s.at[part, n], recv_sem=s2r.at[part, n],
+            device_id={"dp": ((xx + dx) % 4) * 2 + core}, device_id_type=MESH,
         )
+
+    low, high = pl.ds(0, 128), pl.ds(128, 128)
+
+    def hops(part, k):
+        recv, half, got = ((r1d, hd, r2d), (r1g, hg, r2g))[part]
+        block = recv.at[chunk(k)]
+        if k == 0:
+            return (
+                to_chip(block.at[low], half.at[0], part, 0, 1),
+                to_chip(block.at[high], half.at[1], part, 1, 3),
+            )
+        return (to_chip(block, got.at[k - 1], part, 1 + k, (1, 3)[k - 1]),)
+
+    def pass_on(part, k):
+        own, recv, half = ((ownd, r1d, hd), (owng, r1g, hg))[part]
+        q = chunk(k)
+        to_core(recv, recv, part, q).wait_recv()
+        if k == 0:
+            recv[q] = (own[q] + recv[q].astype(F32)).astype(BF)
+        else:
+            hops(part, 0)[k - 1].wait_recv()
+            plain, added = ((high, low), (low, high))[k - 1]
+            recv[q, plain] = (own[q, plain] + recv[q, plain].astype(F32)).astype(BF)
+            recv[q, added] = (
+                own[q, added] + recv[q, added].astype(F32) + half[k - 1].astype(F32)
+            ).astype(BF)
+        for hop in hops(part, k):
+            hop.start()
+
+    def down_grads(i):
+        q = chunk(i)
+        s1d[q] = dot_tn(call[q, :, other], hid[...]).astype(BF)
+        to_core(s1d, r1d, 0, q).start()
+        ownd[q] = dot_tn(call[q, :, mine], hid[...])
 
     def backward_in(i):
         q = chunk(i)
@@ -246,43 +295,35 @@
         call[q, 0:384, 0:384] = main.astype(BF)
         call[q, 0:384, 384:512] = last.astype(BF)
         gh[...] += dot_nt(call[q], wd[q])
-        s1d[q] = dot_tn(call[q, :, other], hid[...]).astype(BF)
-        to_core(s1d, r1d, 0, q).start()
-        ownd[q] = dot_tn(call[q, :, mine], hid[...])
+
+        @pl.when(i < 3)
+        def _():
+            down_grads(i)
+
+        for k in range(2):
+            pl.when(i == k + 1)(functools.partial(pass_on, 0, k))
 
     loop(NQ, backward_in)
 
     def activate_back(r):
         rows = pl.ds(pl.multiple_of(r * 64, 64), 64)
-        act = gacc[rows, :]
         grad = gh[rows, :]
-        sigma = jax.nn.sigmoid(act)
-        gb[rows, :] = (grad * uacc[rows, :] * (sigma * (1.0 + act * (1.0 - sigma)))).astype(BF)
-        ub[rows, :] = (grad * (act * sigma)).astype(BF)
+        gb[rows, :] = (grad * gacc[rows, :]).astype(BF)
+        ub[rows, :] = (grad * uacc[rows, :]).astype(BF)
 
     loop(8, activate_back)
 
     def backward_out(i):
         q = chunk(i)
         sent(sb, 1, q)
-        back = dot_nt(gb[...], wg[q]) + dot_nt(ub[...], wu[q])
-        routed = back[0:384].astype(BF)
+        routed = (dot_nt(gb[0:384, :], wg[q]) + dot_nt(ub[0:384, :], wu[q])).astype(BF)
         pack(sb, q, routed[:, 0:384], routed[:, 384:512])
         exchange(sb, rb, 3, q, -1)
-        locb[q] = back[384:512]
-
-    loop(NQ, backward_out)
-
-    def pass_on(own, recv, dst, part, i):
-        q = chunk(i)
-        to_core(recv, recv, part, q).wait_recv()
-        recv[q] = (own[q] + recv[q].astype(F32)).astype(BF)
-        to_chip(recv, dst, part, i).start()
-
-    loop(3, lambda i: pass_on(ownd, r1d, r2d, 0, i))
-
-    def weight_grads(i):
-        q = chunk(i)
+
+        @pl.when(i == 0)
+        def _():
+            pass_on(0, 2)
+
         away = xall[q, :, other]
         s1g[q, :, 0:768] = dot_tn(away, gb[...]).astype(BF)
         s1g[q, :, 768:1536] = dot_tn(away, ub[...]).astype(BF)
@@ -291,11 +332,29 @@
         owng[q, :, 0:768] = dot_tn(here, gb[...])
         owng[q, :, 768:1536] = dot_tn(here, ub[...])
 
-        @pl.when(i > 0)
+        @pl.when(i == 0)
         def _():
-            pass_on(owng, r1g, r2g, 1, i - 1)
-
-    loop(NQ, weight_grads)
+            down_grads(3)
+
+        for k in range(3):
+            pl.when(i == k + 1)(functools.partial(pass_on, 1, k))
+        locb[q] = dot_nt(gb[384:512, :], wg[q]) + dot_nt(ub[384:512, :], wu[q])
+
+    loop(NQ, backward_out)
+
+    def total(part):
+        own, recv, got = ((ownd, r1d, r2d), (owng, r1g, r2g))[part]
+        to_core(recv, recv, part, xx).wait_recv()
+        own[xx] = own[xx] + recv[xx].astype(F32)
+        hops(part, 1)[0].wait_recv()
+        hops(part, 2)[0].wait_recv()
+        own[xx] = (own[xx] + got[0].astype(F32) + got[1].astype(F32)) * 0.125
+        width = 768 * (1 + part)
+        copy = pltpu.make_async_copy(
+            own.at[xx], ograd_hbm.at[:, pl.ds(1536 * (1 - part), width)], st_sem.at[4 + part]
+        )
+        copy.start()
+        return copy
 
     def finish(i):
         q = chunk(i)
@@ -306,21 +365,10 @@
         cols = pl.ds(pl.multiple_of(q * 512, 512), 512)
         pltpu.make_async_copy(tokout.at[q], otok_hbm.at[:, cols], st_sem.at[q]).start()
 
-    loop(NQ, finish)
-
-    def total(own, recv, got, part):
-        to_core(recv, recv, part, xx).wait_recv()
-        own[xx] = own[xx] + recv[xx].astype(F32)
-        for i in range(3):
-            to_chip(recv, got, part, i).wait_recv()
-        own[xx] = (own[xx] + got[0].astype(F32) + got[1].astype(F32) + got[2].astype(F32)) * 0.125
-
-    total(ownd, r1d, r2d, 0)
-    out_d = pltpu.make_async_copy(ownd.at[xx], ograd_hbm.at[:, pl.ds(1536, 768)], st_sem.at[4])
-    out_d.start()
-    total(owng, r1g, r2g, 1)
-    out_g = pltpu.make_async_copy(owng.at[xx], ograd_hbm.at[:, pl.ds(0, 1536)], st_sem.at[5])
-    out_g.start()
+    out_d = total(0)
+    loop(3, finish)
+    out_g = total(1)
+    finish(3)
 
     def drain(i):
         q = chunk(i)
@@ -332,17 +380,15 @@
         pltpu.make_async_copy(tokout.at[q], otok_hbm.at[:, cols], st_sem.at[q]).wait()
 
     loop(NQ, drain)
-    for i in range(3):
-        to_chip(r1d, r2d, 0, i).wait_send()
-        to_chip(r1g, r2g, 1, i).wait_send()
+    for part in range(2):
+        for k in range(3):
+            for hop in hops(part, k):
+                hop.wait_send()
     out_d.wait()
     out_g.wait()
 
 
 def on_device(tokens, routes, gates, keep, cotangent, w_gate, w_up, w_down):
-    aux = jnp.concatenate(
-        [routes.astype(F32), gates, keep.astype(F32)[:, None]], axis=1
-    )
     hbm = pl.BlockSpec(memory_space=pl.ANY)
     vmem = pl.BlockSpec(memory_space=pltpu.VMEM)
     sem = pltpu.SemaphoreType.DMA
@@ -352,7 +398,7 @@
             jax.ShapeDtypeStruct((128, 2048), BF),
             jax.ShapeDtypeStruct((256, 2304), F32),
         ),
-        in_specs=[vmem] + [hbm] * 5,
+        in_specs=[vmem] * 3 + [hbm] * 5,
         out_specs=(hbm, hbm),
         scratch_shapes=[
             pltpu.VMEM((4, 512, 512), BF),
@@ -383,15 +429,17 @@
             pltpu.VMEM((4, 256, 1536), BF),
             pltpu.VMEM((4, 256, 768), BF),
             pltpu.VMEM((4, 256, 1536), BF),
-            pltpu.VMEM((3, 256, 768), BF),
-            pltpu.VMEM((3, 256, 1536), BF),
+            pltpu.VMEM((2, 256, 768), BF),
+            pltpu.VMEM((2, 256, 1536), BF),
+            pltpu.VMEM((2, 128, 768), BF),
+            pltpu.VMEM((2, 128, 1536), BF),
             sem((5, 4)), sem((6,)), sem((4, 4)), sem((4, 4)),
-            sem((2, 4)), sem((2, 4)), sem((2, 3)), sem((2, 3)),
+            sem((2, 4)), sem((2, 4)), sem((2, 4)), sem((2, 4)),
         ],
         compiler_params=pltpu.CompilerParams(
             collective_id=0, has_side_effects=True, vmem_limit_bytes=67043328
         ),
-    )(aux, tokens, cotangent, w_gate[0], w_up[0], w_down[0])
+    )(routes.T, gates.T, keep.reshape(1, 128), tokens, cotangent, w_gate[0], w_up[0], w_down[0])
     return token_grads, expert_grads[None]
 
 

time: 195 us -> 173 us (0.89)
  Pallas kernels: 185 us -> 167 us
  other arithmetic: 2.03 us -> 0 us
    pallas_call x1, Pallas kernels: 185 us -> 167 us  [on_device(): pl.pallas_call(kernel, out_shape=(jax.ShapeDtypeStruct((128, 2048), BF),...]
where the time goes in v1:
time: 173 us; the launch traced here: 172 us
  Pallas kernels  167 us (97%)
  local copies, waits for them, and re-layouts  5.1 us (3%)
    pallas_call x1, Pallas kernels, on_device(): pl.pallas_call(kernel, out_shape=(jax.ShapeDtypeStruct((128, 2048), BF),...  167 us
    unnamed x2, local copies, waits for them, and re-layouts  5.1 us

profile of v1, /device:TPU:6, one launch (start us, length us, event | category | flops | bytes accessed | tf_op | source)
XLA Modules:
  0.0 172.3 jit_solution(13371940929757362527)
XLA Ops:
  0.6 166.6 %shard_map.95 = (bf16[128,2048]{1,0:T(8,128)(2,1)}, f32[256,2304]{1,0:T(8,128)}) custom-call(s32[2,128]{1,0:T(2,128)} %bitcast.11, f32[2,128]{1,0:T(2,128)} %bitcast.12, s32[1,128]{1,0:T(1,128)} %bitcast.13, bf16[128,2048]{1,0:T(8,128)(2,1)} %tok_hbm.1, bf16[128,2048]{1,0:T(8,128)(2,1)} %cot_hbm.1, bf16[2048,768]{1,0:T(8,128)(2,1)} %bitcast.7, ...), custom_call_target="tpu_custom_call" | custom-call | tf_op jit(solution)/shard_map/pallas_call | solution.py:395
  167.2 1.9 %copy.12 = bf16[128,2048]{1,0:T(8,128)(2,1)} copy(bf16[128,2048]{1,0:T(8,128)(2,1)} %get-tuple-element.8) | data formatting | bytes 1048576
  169.1 3.2 %copy.13 = f32[1,256,2304]{2,1,0:T(8,128)} copy(f32[1,256,2304]{2,1,0:T(8,128)} %bitcast.10) | data formatting | bytes 4718592

commit v2 on v1

--- a/solution.py
+++ b/solution.py
@@ -31,6 +31,10 @@
     return jnp.where(mask, 1.0, 0.0).astype(BF)
 
 
+def pair(g):
+    return pl.ds(256 * g, 256), pl.ds(192 * g, 192)
+
+
 def iota(shape, axis):
     return lax.broadcasted_iota(jnp.int32, shape, axis)
 
@@ -45,11 +49,11 @@
 
 def kernel(
     routes_ref, gates_ref, keep_ref, tok_hbm, cot_hbm, wg_hbm, wu_hbm, wd_hbm,
-    otok_hbm, ograd_hbm,
-    xall, call, cot, wg, wu, wd, gacc, uacc, hid, gh, gb, ub, locb, tokout,
+    otok, ograd,
+    xall, call, cot, wg, wu, wd, gacc, uacc, hid, gh, gb, ub, locb,
     lmat, dmat, umat, pmat, sa, ra, sb, rb,
     ownd, owng, s1d, s1g, r1d, r1g, r2d, r2g, hd, hg,
-    ld_sem, st_sem, ssem, rsem, s1s, s1r, s2s, s2r,
+    ld_sem, ssem, rsem, s1s, s1r, s2s, s2r,
 ):
     me = lax.axis_index("expert")
     dp = lax.axis_index("dp")
@@ -112,22 +116,31 @@
             lmat[j, :, pl.ds(256 * k, 128)] = onehot(iota((512, 128), 0) == rows[0])
             lmat[j, :, pl.ds(256 * k + 128, 128)] = onehot(iota((512, 128), 0) == rows[1 + j])
 
-    def exchange(src, dst, a, q, sign):
-        for p in range(32):
+    def exchange(src, dst, a, q, g, sign):
+        for p in range(16 * g, 16 * g + 16):
             dz, dy = ORDER[p // 4], p % 4
             block = pl.ds(16 * p, 16)
             if p == SELF:
-                pltpu.make_async_copy(src.at[q, block], dst.at[q, block], rsem.at[a, q]).start()
+                pltpu.make_async_copy(src.at[q, block], dst.at[q, block], rsem.at[a, q, g]).start()
             else:
                 to = ((z + sign * dz + 8) % 8) * 4 + (y + sign * dy + 4) % 4
                 pltpu.make_async_remote_copy(
                     src_ref=src.at[q, block], dst_ref=dst.at[q, block],
-                    send_sem=ssem.at[a, q], recv_sem=rsem.at[a, q],
+                    send_sem=ssem.at[a, q], recv_sem=rsem.at[a, q, g],
                     device_id={"expert": to}, device_id_type=MESH,
                 ).start()
 
-    def arrived(dst, a, q):
-        pltpu.make_async_copy(dst.at[q], dst.at[q], rsem.at[a, q]).wait()
+    def exchange_all(src, dst, a, q, sign):
+        exchange(src, dst, a, q, 0, sign)
+        exchange(src, dst, a, q, 1, sign)
+
+    def arrived(dst, a, q, g):
+        part = dst.at[q, pair(g)[0]]
+        pltpu.make_async_copy(part, part, rsem.at[a, q, g]).wait()
+
+    def arrived_all(dst, a, q):
+        arrived(dst, a, q, 0)
+        arrived(dst, a, q, 1)
 
     def sent(src, a, q):
         part = src.at[q, pl.ds(0, 496)]
@@ -141,12 +154,18 @@
             )
             dst[q, :, part] = dot(lmat[j], stack).astype(BF)
 
-    def gather(mat, src, q):
-        main = dot(mat[0], src[q])
-        last = dot(mat[1], src[q, :, 0:128])
-        last += dot(mat[2], src[q, :, 128:256])
-        last += dot(mat[3], src[q, :, 256:384])
+    def gather(mat, src):
+        main = dot(mat[0], src[...])
+        last = dot(mat[1], src[:, 0:128])
+        last += dot(mat[2], src[:, 128:256])
+        last += dot(mat[3], src[:, 256:384])
         return main, last
+
+    def unpack(dst, src, q, g):
+        packed, plain = pair(g)
+        main, last = gather(umat, src.at[q, packed])
+        dst[q, plain, 0:384] = main.astype(BF)
+        dst[q, plain, 384:512] = last.astype(BF)
 
     def dispatch(i):
         q = chunk(i)
@@ -156,58 +175,72 @@
 
     loop(NQ, dispatch)
     pl.semaphore_wait(bar, 35)
-    loop(NQ, lambda i: exchange(sa, ra, 0, chunk(i), 1))
-
-    row = iota((384, 512), 0)
-    col = iota((384, 512), 1)
+    for g in range(2):
+        loop(NQ, lambda i: exchange(sa, ra, 0, chunk(i), g, 1))
+
+    row = iota((192, 256), 0)
+    col = iota((192, 256), 1)
     blk = (row * 43691) >> 19
     s = row - 12 * blk
     umat[0] = onehot(col == 16 * blk + s)
     for j in range(3):
         umat[1 + j] = onehot((col == 16 * blk + 12 + (s & 3)) & ((s >> 2) == j))
-    row = iota((512, 384), 0)
-    col = iota((512, 384), 1)
+    row = iota((256, 192), 0)
+    col = iota((256, 192), 1)
     s = row & 15
     pmat[0] = onehot((s < 12) & (col == 12 * (row >> 4) + s))
     for j in range(3):
         pmat[1 + j] = onehot((s >= 12) & (col == 12 * (row >> 4) + 4 * j + s - 12))
 
-    def pack(dst, q, main, last):
+    def pack(dst, q, g, rows):
+        packed = pair(g)[0]
         for j in range(3):
             part = slice(128 * j, 128 * j + 128)
-            dst[q, :, part] = (dot(pmat[0], main[:, part]) + dot(pmat[1 + j], last)).astype(BF)
+            dst[q, packed, part] = (dot(pmat[0], rows[:, part]) + dot(pmat[1 + j], rows[:, 384:])).astype(BF)
 
     gacc[...] = jnp.zeros_like(gacc)
     uacc[...] = jnp.zeros_like(uacc)
 
-    def forward_in(i):
-        q = chunk(i)
-        load(1, q).wait()
-        load(2, q).wait()
-        arrived(ra, 0, q)
-        main, last = gather(umat, ra, q)
-        xall[q, 0:384, 0:384] = main.astype(BF)
-        xall[q, 0:384, 384:512] = last.astype(BF)
-        gacc[...] += dot(xall[q], wg[q])
-        uacc[...] += dot(xall[q], wu[q])
-
-    loop(NQ, forward_in)
+    def project(q, rows):
+        gacc[rows, :] += dot(xall[q, rows, :], wg[q])
+        uacc[rows, :] += dot(xall[q, rows, :], wu[q])
 
     def activate(r):
         rows = pl.ds(pl.multiple_of(r * 64, 64), 64)
         act = gacc[rows, :]
         hid[rows, :] = (act * jax.nn.sigmoid(act) * uacc[rows, :]).astype(BF)
 
-    loop(8, activate)
-
-    def forward_out(i):
-        q = chunk(i)
-        load(3, q).wait()
-        result = dot(hid[0:384, :], wd[q]).astype(BF)
-        pack(sb, q, result[:, 0:384], result[:, 384:512])
-        exchange(sb, rb, 1, q, -1)
-
-    loop(NQ, forward_out)
+    def local_in(i):
+        q = chunk(i)
+        load(1, q).wait()
+        load(2, q).wait()
+        project(q, pl.ds(384, 128))
+
+    loop(NQ, local_in)
+    loop(2, lambda r: activate(r + 6))
+
+    def group(g):
+        plain = pair(g)[1]
+
+        def forward_in(i):
+            q = chunk(i)
+            arrived(ra, 0, q, g)
+            unpack(xall, ra, q, g)
+            project(q, plain)
+
+        def forward_out(i):
+            q = chunk(i)
+            if g == 0:
+                load(3, q).wait()
+            pack(sb, q, g, dot(hid[plain, :], wd[q]).astype(BF))
+            exchange(sb, rb, 1, q, g, -1)
+
+        loop(NQ, forward_in)
+        loop(3, lambda r: activate(r + 3 * g))
+        loop(NQ, forward_out)
+
+    group(0)
+    group(1)
 
     def factors(r):
         rows = pl.ds(pl.multiple_of(r * 64, 64), 64)
@@ -226,14 +259,14 @@
         load(4, q).wait()
         local = keep * dot(hid[384:512, :], wd[q])
         sent(sa, 0, q)
-        arrived(rb, 1, q)
-        main, last = gather(dmat, rb, q)
+        arrived_all(rb, 1, q)
+        main, last = gather(dmat, rb.at[q])
         picked = jnp.concatenate([main, last], axis=1)
         mixed = gates[0] * picked[0:128] + gates[1] * picked[128:256]
         difference = mixed - local
         upstream = cot[q].astype(F32) + difference
         scatter(sa, q, (gates[0] * upstream).astype(BF), (gates[1] * upstream).astype(BF))
-        exchange(sa, ra, 2, q, 1)
+        exchange_all(sa, ra, 2, q, 1)
         call[q, 384:512, :] = (-(keep * difference)).astype(BF)
 
     loop(NQ, turn)
@@ -290,10 +323,9 @@
 
     def backward_in(i):
         q = chunk(i)
-        arrived(ra, 2, q)
-        main, last = gather(umat, ra, q)
-        call[q, 0:384, 0:384] = main.astype(BF)
-        call[q, 0:384, 384:512] = last.astype(BF)
+        for g in range(2):
+            arrived(ra, 2, q, g)
+            unpack(call, ra, q, g)
         gh[...] += dot_nt(call[q], wd[q])
 
         @pl.when(i < 3)
@@ -316,9 +348,10 @@
     def backward_out(i):
         q = chunk(i)
         sent(sb, 1, q)
-        routed = (dot_nt(gb[0:384, :], wg[q]) + dot_nt(ub[0:384, :], wu[q])).astype(BF)
-        pack(sb, q, routed[:, 0:384], routed[:, 384:512])
-        exchange(sb, rb, 3, q, -1)
+        for g in range(2):
+            plain = pair(g)[1]
+            pack(sb, q, g, (dot_nt(gb[plain, :], wg[q]) + dot_nt(ub[plain, :], wu[q])).astype(BF))
+            exchange(sb, rb, 3, q, g, -1)
 
         @pl.when(i == 0)
         def _():
@@ -348,26 +381,19 @@
         own[xx] = own[xx] + recv[xx].astype(F32)
         hops(part, 1)[0].wait_recv()
         hops(part, 2)[0].wait_recv()
-        own[xx] = (own[xx] + got[0].astype(F32) + got[1].astype(F32)) * 0.125
-        width = 768 * (1 + part)
-        copy = pltpu.make_async_copy(
-            own.at[xx], ograd_hbm.at[:, pl.ds(1536 * (1 - part), width)], st_sem.at[4 + part]
-        )
-        copy.start()
-        return copy
-
+        columns = pl.ds(1536 * (1 - part), 768 * (1 + part))
+        ograd[:, columns] = (own[xx] + got[0].astype(F32) + got[1].astype(F32)) * 0.125
     def finish(i):
         q = chunk(i)
-        arrived(rb, 3, q)
-        main, last = gather(dmat, rb, q)
+        arrived_all(rb, 3, q)
+        main, last = gather(dmat, rb.at[q])
         picked = jnp.concatenate([main, last], axis=1)
-        tokout[q] = (picked[0:128] + picked[128:256] + locb[q]).astype(BF)
         cols = pl.ds(pl.multiple_of(q * 512, 512), 512)
-        pltpu.make_async_copy(tokout.at[q], otok_hbm.at[:, cols], st_sem.at[q]).start()
-
-    out_d = total(0)
+        otok[:, cols] = (picked[0:128] + picked[128:256] + locb[q]).astype(BF)
+
+    total(0)
     loop(3, finish)
-    out_g = total(1)
+    total(1)
     finish(3)
 
     def drain(i):
@@ -376,16 +402,12 @@
         sent(sb, 3, q)
         to_core(s1d, r1d, 0, q).wait_send()
         to_core(s1g, r1g, 1, q).wait_send()
-        cols = pl.ds(pl.multiple_of(q * 512, 512), 512)
-        pltpu.make_async_copy(tokout.at[q], otok_hbm.at[:, cols], st_sem.at[q]).wait()
 
     loop(NQ, drain)
     for part in range(2):
         for k in range(3):
             for hop in hops(part, k):
                 hop.wait_send()
-    out_d.wait()
-    out_g.wait()
 
 
 def on_device(tokens, routes, gates, keep, cotangent, w_gate, w_up, w_down):
@@ -395,11 +417,11 @@
     token_grads, expert_grads = pl.pallas_call(
         kernel,
         out_shape=(
-            jax.ShapeDtypeStruct((128, 2048), BF),
-            jax.ShapeDtypeStruct((256, 2304), F32),
+            pltpu.VMEM((128, 2048), BF),
+            pltpu.VMEM((256, 2304), F32),
         ),
         in_specs=[vmem] * 3 + [hbm] * 5,
-        out_specs=(hbm, hbm),
+        out_specs=(vmem, vmem),
         scratch_shapes=[
             pltpu.VMEM((4, 512, 512), BF),
             pltpu.VMEM((4, 512, 512), BF),
@@ -414,11 +436,10 @@
             pltpu.VMEM((512, 768), BF),
             pltpu.VMEM((512, 768), BF),
             pltpu.VMEM((4, 128, 512), F32),
-            pltpu.VMEM((4, 128, 512), BF),
             pltpu.VMEM((3, 512, 512), BF),
             pltpu.VMEM((4, 256, 512), BF),
-            pltpu.VMEM((4, 384, 512), BF),
-            pltpu.VMEM((4, 512, 384), BF),
+            pltpu.VMEM((4, 192, 256), BF),
+            pltpu.VMEM((4, 256, 192), BF),
             pltpu.VMEM((4, 512, 384), BF),
             pltpu.VMEM((4, 512, 384), BF),
             pltpu.VMEM((4, 512, 384), BF),
@@ -433,11 +454,11 @@
             pltpu.VMEM((2, 256, 1536), BF),
             pltpu.VMEM((2, 128, 768), BF),
             pltpu.VMEM((2, 128, 1536), BF),
-            sem((5, 4)), sem((6,)), sem((4, 4)), sem((4, 4)),
+            sem((5, 4)), sem((4, 4)), sem((4, 4, 2)),
             sem((2, 4)), sem((2, 4)), sem((2, 4)), sem((2, 4)),
         ],
         compiler_params=pltpu.CompilerParams(
-            collective_id=0, has_side_effects=True, vmem_limit_bytes=67043328
+            collective_id=0, has_side_effects=True, vmem_limit_bytes=60 * 2**20
         ),
     )(routes.T, gates.T, keep.reshape(1, 128), tokens, cotangent, w_gate[0], w_up[0], w_down[0])
     return token_grads, expert_grads[None]

time: 173 us -> 159 us (0.919)
  Pallas kernels: 167 us -> 156 us
  local copies, waits for them, and re-layouts: 5.1 us -> 2.2 us
    pallas_call x1, Pallas kernels: 167 us -> 156 us  [on_device(): pl.pallas_call(kernel, out_shape=(pltpu.VMEM((128, 2048), BF), pltpu.VMEM...]
    unnamed x2, local copies, waits for them, and re-layouts: 5.1 us -> 2.2 us
where the time goes in v2:
time: 159 us
  Pallas kernels  156 us (98%)
  local copies, waits for them, and re-layouts  2.2 us (1%)
    pallas_call x1, Pallas kernels, on_device(): pl.pallas_call(kernel, out_shape=(pltpu.VMEM((128, 2048), BF), pltpu.VMEM...  156 us

profile of v2, /device:TPU:6, one launch (start us, length us, event | category | flops | bytes accessed | tf_op | source)
XLA Modules:
  0.0 159.3 jit_solution(14911043659686356907)
XLA Ops:
  0.6 156.5 %shard_map.95 = (bf16[128,2048]{1,0:T(8,128)(2,1)S(1)}, f32[256,2304]{1,0:T(8,128)S(1)}) custom-call(s32[2,128]{1,0:T(2,128)} %bitcast.11, f32[2,128]{1,0:T(2,128)} %bitcast.12, s32[1,128]{1,0:T(1,128)} %bitcast.13, bf16[128,2048]{1,0:T(8,128)(2,1)} %tok_hbm.1, bf16[128,2048]{1,0:T(8,128)(2,1)} %cot_hbm.1, bf16[2048,768]{1,0:T(8,128)(2,1)} %bitcast.8, ...), custom_call_target="tpu_custom_call" | custom-call | tf_op jit(solution)/shard_map/pallas_call | solution.py:417
  157.1 0.8 copy.12
  157.9 1.4 copy.13

commit v3 on v2

--- a/solution.py
+++ b/solution.py
@@ -130,10 +130,6 @@
                     device_id={"expert": to}, device_id_type=MESH,
                 ).start()
 
-    def exchange_all(src, dst, a, q, sign):
-        exchange(src, dst, a, q, 0, sign)
-        exchange(src, dst, a, q, 1, sign)
-
     def arrived(dst, a, q, g):
         part = dst.at[q, pair(g)[0]]
         pltpu.make_async_copy(part, part, rsem.at[a, q, g]).wait()
@@ -266,7 +262,8 @@
         difference = mixed - local
         upstream = cot[q].astype(F32) + difference
         scatter(sa, q, (gates[0] * upstream).astype(BF), (gates[1] * upstream).astype(BF))
-        exchange_all(sa, ra, 2, q, 1)
+        exchange(sa, ra, 2, q, 0, 1)
+        exchange(sa, ra, 2, q, 1, 1)
         call[q, 384:512, :] = (-(keep * difference)).astype(BF)
 
     loop(NQ, turn)
@@ -297,23 +294,33 @@
                 to_chip(block.at[low], half.at[0], part, 0, 1),
                 to_chip(block.at[high], half.at[1], part, 1, 3),
             )
-        return (to_chip(block, got.at[k - 1], part, 1 + k, (1, 3)[k - 1]),)
+        land = got.at[k - 1]
+        return tuple(
+            to_chip(block.at[rows], land.at[rows], part, 2 * k + n, (1, 3)[k - 1])
+            for n, rows in enumerate(((high, low), (low, high))[k - 1])
+        )
 
     def pass_on(part, k):
-        own, recv, half = ((ownd, r1d, hd), (owng, r1g, hg))[part]
+        own, recv = ((ownd, r1d), (owng, r1g))[part]
         q = chunk(k)
         to_core(recv, recv, part, q).wait_recv()
         if k == 0:
             recv[q] = (own[q] + recv[q].astype(F32)).astype(BF)
+            for hop in hops(part, k):
+                hop.start()
         else:
-            hops(part, 0)[k - 1].wait_recv()
             plain, added = ((high, low), (low, high))[k - 1]
             recv[q, plain] = (own[q, plain] + recv[q, plain].astype(F32)).astype(BF)
-            recv[q, added] = (
-                own[q, added] + recv[q, added].astype(F32) + half[k - 1].astype(F32)
-            ).astype(BF)
-        for hop in hops(part, k):
-            hop.start()
+            hops(part, k)[0].start()
+            own[q, added] = own[q, added] + recv[q, added].astype(F32)
+
+    def pass_sum(part, k):
+        own, recv, half = ((ownd, r1d, hd), (owng, r1g, hg))[part]
+        q = chunk(k)
+        added = (low, high)[k - 1]
+        hops(part, 0)[k - 1].wait_recv()
+        recv[q, added] = (own[q, added] + half[k - 1].astype(F32)).astype(BF)
+        hops(part, k)[1].start()
 
     def down_grads(i):
         q = chunk(i)
@@ -321,21 +328,8 @@
         to_core(s1d, r1d, 0, q).start()
         ownd[q] = dot_tn(call[q, :, mine], hid[...])
 
-    def backward_in(i):
-        q = chunk(i)
-        for g in range(2):
-            arrived(ra, 2, q, g)
-            unpack(call, ra, q, g)
-        gh[...] += dot_nt(call[q], wd[q])
-
-        @pl.when(i < 3)
-        def _():
-            down_grads(i)
-
-        for k in range(2):
-            pl.when(i == k + 1)(functools.partial(pass_on, 0, k))
-
-    loop(NQ, backward_in)
+    def hidden_grads(q, rows):
+        gh[rows, :] += dot_nt(call[q, rows, :], wd[q])
 
     def activate_back(r):
         rows = pl.ds(pl.multiple_of(r * 64, 64), 64)
@@ -343,20 +337,20 @@
         gb[rows, :] = (grad * gacc[rows, :]).astype(BF)
         ub[rows, :] = (grad * uacc[rows, :]).astype(BF)
 
-    loop(8, activate_back)
-
-    def backward_out(i):
-        q = chunk(i)
-        sent(sb, 1, q)
-        for g in range(2):
-            plain = pair(g)[1]
-            pack(sb, q, g, (dot_nt(gb[plain, :], wg[q]) + dot_nt(ub[plain, :], wu[q])).astype(BF))
-            exchange(sb, rb, 3, q, g, -1)
-
-        @pl.when(i == 0)
-        def _():
-            pass_on(0, 2)
-
+    def backward_in(g, i):
+        q = chunk(i)
+        arrived(ra, 2, q, g)
+        unpack(call, ra, q, g)
+        hidden_grads(q, pair(g)[1])
+
+    def backward_out(g, i):
+        q = chunk(i)
+        plain = pair(g)[1]
+        pack(sb, q, g, (dot_nt(gb[plain, :], wg[q]) + dot_nt(ub[plain, :], wu[q])).astype(BF))
+        exchange(sb, rb, 3, q, g, -1)
+
+    def weight_grads(i):
+        q = chunk(i)
         away = xall[q, :, other]
         s1g[q, :, 0:768] = dot_tn(away, gb[...]).astype(BF)
         s1g[q, :, 768:1536] = dot_tn(away, ub[...]).astype(BF)
@@ -365,22 +359,55 @@
         owng[q, :, 0:768] = dot_tn(here, gb[...])
         owng[q, :, 768:1536] = dot_tn(here, ub[...])
 
+    loop(NQ, lambda i: hidden_grads(chunk(i), pl.ds(384, 128)))
+    loop(2, lambda r: activate_back(r + 6))
+    loop(NQ, lambda i: sent(sb, 1, chunk(i)))
+
+    def chunks(i):
+        backward_in(0, i)
+        backward_in(1, i)
+        down_grads(i)
+        for k in range(2):
+            pl.when(i == k + 1)(functools.partial(pass_on, 0, k))
+        pl.when(i == 2)(functools.partial(pass_sum, 0, 1))
+
+    loop(3, chunks)
+    pass_on(0, 2)
+    pass_sum(0, 2)
+
+    backward_in(0, 3)
+    loop(3, activate_back)
+    loop(NQ, functools.partial(backward_out, 0))
+    backward_in(1, 3)
+    loop(3, lambda r: activate_back(r + 3))
+
+    def rest(i):
+        weight_grads(i)
+        backward_out(1, i)
+
         @pl.when(i == 0)
         def _():
             down_grads(3)
 
         for k in range(3):
-            pl.when(i == k + 1)(functools.partial(pass_on, 1, k))
+            pl.when(i == k)(functools.partial(pass_on, 1, k))
+
+    loop(NQ, rest)
+
+    def local_back(i):
+        q = chunk(i)
         locb[q] = dot_nt(gb[384:512, :], wg[q]) + dot_nt(ub[384:512, :], wu[q])
 
-    loop(NQ, backward_out)
+    loop(NQ, local_back)
+    pass_sum(1, 1)
+    pass_sum(1, 2)
 
     def total(part):
         own, recv, got = ((ownd, r1d, r2d), (owng, r1g, r2g))[part]
         to_core(recv, recv, part, xx).wait_recv()
         own[xx] = own[xx] + recv[xx].astype(F32)
-        hops(part, 1)[0].wait_recv()
-        hops(part, 2)[0].wait_recv()
+        for hop in hops(part, 1) + hops(part, 2):
+            hop.wait_recv()
         columns = pl.ds(1536 * (1 - part), 768 * (1 + part))
         ograd[:, columns] = (own[xx] + got[0].astype(F32) + got[1].astype(F32)) * 0.125
     def finish(i):
@@ -455,7 +482,7 @@
             pltpu.VMEM((2, 128, 768), BF),
             pltpu.VMEM((2, 128, 1536), BF),
             sem((5, 4)), sem((4, 4)), sem((4, 4, 2)),
-            sem((2, 4)), sem((2, 4)), sem((2, 4)), sem((2, 4)),
+            sem((2, 4)), sem((2, 4)), sem((2, 6)), sem((2, 6)),
         ],
         compiler_params=pltpu.CompilerParams(
             collective_id=0, has_side_effects=True, vmem_limit_bytes=60 * 2**20

time: 159 us -> 156 us (0.981)
  Pallas kernels: 156 us -> 153 us
    pallas_call x1, Pallas kernels: 156 us -> 153 us  [on_device(): pl.pallas_call(kernel, out_shape=(pltpu.VMEM((128, 2048), BF), pltpu.VMEM...]
where the time goes in v3:
time: 156 us
  Pallas kernels  153 us (98%)
  local copies, waits for them, and re-layouts  2.2 us (1%)
    pallas_call x1, Pallas kernels, on_device(): pl.pallas_call(kernel, out_shape=(pltpu.VMEM((128, 2048), BF), pltpu.VMEM...  153 us

profile of v3, /device:TPU:6, one launch (start us, length us, event | category | flops | bytes accessed | tf_op | source)
XLA Modules:
  0.0 155.8 jit_solution(9349722315288422960)
XLA Ops:
  0.6 153.0 %shard_map.95 = (bf16[128,2048]{1,0:T(8,128)(2,1)S(1)}, f32[256,2304]{1,0:T(8,128)S(1)}) custom-call(s32[2,128]{1,0:T(2,128)} %bitcast.11, f32[2,128]{1,0:T(2,128)} %bitcast.12, s32[1,128]{1,0:T(1,128)} %bitcast.13, bf16[128,2048]{1,0:T(8,128)(2,1)} %tok_hbm.1, bf16[128,2048]{1,0:T(8,128)(2,1)} %cot_hbm.1, bf16[2048,768]{1,0:T(8,128)(2,1)} %bitcast.8, ...), custom_call_target="tpu_custom_call" | custom-call | tf_op jit(solution)/shard_map/pallas_call | solution.py:444
  153.6 0.8 copy.12
  154.4 1.4 copy.13

commit v4 on v3

--- a/solution.py
+++ b/solution.py
@@ -377,22 +377,30 @@
 
     backward_in(0, 3)
     loop(3, activate_back)
-    loop(NQ, functools.partial(backward_out, 0))
+    loop(2, functools.partial(backward_out, 0))
     backward_in(1, 3)
     loop(3, lambda r: activate_back(r + 3))
 
     def rest(i):
         weight_grads(i)
-        backward_out(1, i)
 
         @pl.when(i == 0)
         def _():
-            down_grads(3)
+            loop(2, lambda n: backward_out(0, n + 2))
+
+        @pl.when(i > 0)
+        def _():
+            backward_out(1, i)
 
         for k in range(3):
             pl.when(i == k)(functools.partial(pass_on, 1, k))
 
+        @pl.when(i == 0)
+        def _():
+            backward_out(1, 0)
+
     loop(NQ, rest)
+    down_grads(3)
 
     def local_back(i):
         q = chunk(i)
@@ -419,9 +427,8 @@
         otok[:, cols] = (picked[0:128] + picked[128:256] + locb[q]).astype(BF)
 
     total(0)
-    loop(3, finish)
+    loop(NQ, finish)
     total(1)
-    finish(3)
 
     def drain(i):
         q = chunk(i)

time: 156 us -> 157 us (level)
  no operation moved by 1% of the time
where the time goes in v4:
time: 157 us; the launch traced here: 156 us
  Pallas kernels  153 us (97%)
  local copies, waits for them, and re-layouts  2.2 us (1%)
    pallas_call x1, Pallas kernels, on_device(): pl.pallas_call(kernel, out_shape=(pltpu.VMEM((128, 2048), BF), pltpu.VMEM...  153 us

profile of v4, /device:TPU:6, one launch (start us, length us, event | category | flops | bytes accessed | tf_op | source)
XLA Modules:
  0.0 156.2 jit_solution(18268550959162556556)
XLA Ops:
  0.6 153.4 %shard_map.95 = (bf16[128,2048]{1,0:T(8,128)(2,1)S(1)}, f32[256,2304]{1,0:T(8,128)S(1)}) custom-call(s32[2,128]{1,0:T(2,128)} %bitcast.11, f32[2,128]{1,0:T(2,128)} %bitcast.12, s32[1,128]{1,0:T(1,128)} %bitcast.13, bf16[128,2048]{1,0:T(8,128)(2,1)} %tok_hbm.1, bf16[128,2048]{1,0:T(8,128)(2,1)} %cot_hbm.1, bf16[2048,768]{1,0:T(8,128)(2,1)} %bitcast.8, ...), custom_call_target="tpu_custom_call" | custom-call | tf_op jit(solution)/shard_map/pallas_call | solution.py:451
  154.0 0.8 copy.12
  154.8 1.4 copy.13
